TPU v7x, 32 devices: a whole 2x2x4 slice. The times are simulated.
32 devices in a mesh: groups: 2 (over x), ctx: 8 (over z, y), exp: 2 (over core).
Axes of the slice: x: 2, y: 2, z: 4, core: 2. Of those that a mesh axis runs over, the one named last changes fastest.
Arguments:
- tokens: bfloat16 [2048, 5120], P(('groups', 'ctx'), 'exp'), parts along dimension 0, may hold values from -6 to 6
- route_ids: int32 [2048, 2], P(('groups', 'ctx')), parts along dimension 0, may hold values from 0 to 3, all different within a row; in each aligned block of 128 rows (0 to 127, 128 to 255, ...) at most 128 rows name the same one
- route_gates: float32 [2048, 2], P(('groups', 'ctx')), parts along dimension 0, may hold values from 0.2 to 1
- w_in: bfloat16 [8, 5120, 1536], P('ctx', 'exp'), may hold values from -0.078125 to 0.078125
- w_out: bfloat16 [8, 768, 5120], P('ctx', None, 'exp'), may hold values from -0.15625 to 0.15625
Outputs:
- mixed: bfloat16 [2048, 5120], P(('groups', 'ctx'), 'exp'), parts along dimension 0
There are 2 independent parts, one for each index of `groups`. A program takes and returns all parts, laid end to end along the dimension named above; an argument that names none is the same for every part. Nothing has to cross between parts.
Inputs may be any that keep to these rules, and one draw needn't show every extreme that they name: `route_ids`: within the 128 rows of one device no expert is named more than 128 times, a bound that some block reaches; the ids of one token differ.
All inputs are finite; a program needn't handle non-finite values.
Results may differ from a plain program's by a relative error of at most 0.025.
Values may be sent and summed in bfloat16 or wider, within the bound.
A program may use at most 64 MiB of HBM per device.

v0:
```python
import jax
import jax.numpy as jnp
from jax import lax
from jax.sharding import PartitionSpec as P


def expert_half(rows, w_in, w_out):
    gate_up = jnp.dot(rows, w_in[0], preferred_element_type=jnp.float32)
    summed = lax.psum(gate_up.astype(jnp.bfloat16), "exp").astype(jnp.float32)
    hidden_units = w_out.shape[1]
    hidden = (jax.nn.silu(summed[:, :hidden_units]) * summed[:, hidden_units:]).astype(jnp.bfloat16)
    return jnp.dot(hidden, w_out[0], preferred_element_type=jnp.float32).astype(jnp.bfloat16)


def per_device(tokens, route_ids, route_gates, w_in, w_out):
    ctx_size = lax.axis_size("ctx")
    experts = ctx_size // 2
    tok_rows, half_width = tokens.shape
    top_count = route_ids.shape[1]
    capacity = 2 * ((top_count * tok_rows + experts - 1) // experts)
    slots = experts * capacity
    flat_ids = route_ids.reshape(-1)
    onehot = (flat_ids[:, None] == jnp.arange(experts, dtype=jnp.int32)[None, :]).astype(jnp.int32)
    before = jnp.cumsum(onehot, axis=0) - onehot
    rank = jnp.sum(before * onehot, axis=1)
    slot_of = flat_ids * capacity + rank
    placed = (slot_of[:, None] == jnp.arange(slots, dtype=jnp.int32)[None, :]).astype(jnp.bfloat16)
    placed = placed.reshape(tok_rows, top_count, slots)
    every_map = jnp.sum(placed.astype(jnp.float32), axis=1).astype(jnp.bfloat16)
    gathered = lax.dot_general(
        every_map, tokens, (((0,), (0,)), ((), ())), preferred_element_type=jnp.float32
    ).astype(jnp.bfloat16)
    outgoing = jnp.broadcast_to(
        gathered.reshape(experts, 1, capacity, half_width), (experts, 2, capacity, half_width)
    ).reshape(ctx_size, capacity, half_width)
    received = lax.all_to_all(outgoing, "ctx", split_axis=0, concat_axis=0, tiled=True)
    count = received.shape[1]
    partial_out = expert_half(received.reshape(-1, half_width), w_in, w_out).reshape(
        ctx_size, count, half_width
    )
    returned = lax.all_to_all(partial_out, "ctx", split_axis=0, concat_axis=0, tiled=True)
    results = (
        jnp.sum(returned.astype(jnp.float32).reshape(experts, 2, capacity, half_width), axis=1)
        .astype(jnp.bfloat16)
        .reshape(slots, half_width)
    )
    mixed = jnp.zeros((tok_rows, half_width), jnp.float32)
    for route in range(top_count):
        route_out = jnp.dot(placed[:, route], results, preferred_element_type=jnp.float32)
        mixed = mixed + route_gates[:, route : route + 1] * route_out
    return mixed.astype(jnp.bfloat16)


def solution(mesh):
    placed = (
        P(("groups", "ctx"), "exp"),
        P(("groups", "ctx"), None),
        P(("groups", "ctx"), None),
        P("ctx", "exp", None),
        P("ctx", None, "exp"),
    )
    return jax.shard_map(
        per_device,
        mesh=mesh,
        in_specs=placed,
        out_specs=P(("groups", "ctx"), "exp"),
        check_vma=False,
    )
```

profile of v0, /device:TPU:8, one launch (start us, length us, event | category | flops | bytes accessed | tf_op | source)
XLA Modules:
  0.0 306.8 jit_solution(16973427262599416705)
XLA Ops:
  6.5 0.8 copy.16
  7.4 0.1 eq.44
  7.5 0.1 eq.40
  7.7 1.2 reduce-window.6
  8.9 0.1 slice.32
  9.0 0.1 copy.18
  9.1 0.1 copy.19
  9.3 0.1 reduce_sum.33
  9.5 0.7 multiply_add_fusion
  10.2 0.1 convert_reduce_fusion
  10.4 0.9 convolution_convert_fusion.1
  11.3 0.4 broadcast_in_dim.5
  11.7 121.0 %all_to_all.10 = bf16[8,128,2560]{2,1,0:T(8,128)(2,1)S(1)} all-to-all(bf16[8,128,2560]{2,1,0:T(8,128)(2,1)S(1)} %bitcast.51), channel_id=1, replica_groups=mesh['groups'=2,'ctx'=8,'exp'=2] {'ctx'}, dimensions={0} | all-to-all | bytes 10485760 | tf_op jit(solution)/shard_map/all_to_all | solution.py:36
  132.8 9.7 %fusion.3 = bf16[1024,1536]{1,0:T(8,128)(2,1)} fusion(bf16[1024,2560]{1,0:T(8,128)(2,1)S(1)} %bitcast.54, bf16[1,2560,1536]{2,1,0:T(8,128)(2,1)S(1)} %bitcast.57), kind=kOutput, calls=%fused_computation.6 | convolution fusion | flops 8054636544 | bytes 16252928 | tf_op jit(solution)/shard_map/dot_general | solution.py:8
  142.5 23.2 %all-reduce.2.cloned.1.call-done = bf16[1024,1536]{1,0:T(8,128)(2,1)} async-done(((bf16[1024,1536]{1,0:T(8,128)(2,1)}), bf16[1024,1536]{1,0:T(8,128)(2,1)}) %all-reduce.2.cloned.1.call-update) | async-done | bytes 3145744 | tf_op jit(solution)/shard_map/psum | solution.py:9
  165.6 2.9 convert_element_type.54
  168.5 0.2 copy-done.2
  168.7 6.1 %convolution_convert_fusion = bf16[1024,2560]{1,0:T(8,128)(2,1)} fusion(bf16[1,768,2560]{2,1,0:T(8,128)(2,1)S(1)} %copy-done.2, f32[1024,1536]{1,0:T(8,128)S(1)} %convert_element_type.54), kind=kOutput, calls=%fused_computation.2 | convolution fusion | flops 4033871872 | bytes 15466496 | tf_op jit(solution)/shard_map/dot_general | solution.py:12
  174.8 6.2 %all-to-all-start.1 = ((bf16[8,128,2560]{2,1,0:T(8,128)(2,1)}), bf16[8,128,2560]{2,1,0:T(8,128)(2,1)}, u32[]{:S(2)}, u32[]{:S(2)}) async-start(bf16[8,128,2560]{2,1,0:T(8,128)(2,1)} %bitcast.53), calls=%async_computation.1 | async-start | bytes 10485760 | tf_op jit(solution)/shard_map/all_to_all | solution.py:41
  181.0 0.1 iota_compare_fusion
  181.1 113.5 %all-to-all-done.1 = bf16[8,128,2560]{2,1,0:T(8,128)(2,1)} async-done(((bf16[8,128,2560]{2,1,0:T(8,128)(2,1)}), bf16[8,128,2560]{2,1,0:T(8,128)(2,1)}, u32[]{:S(2)}, u32[]{:S(2)}) %all-to-all-start.1) | async-done | bytes 5242912 | tf_op jit(solution)/shard_map/all_to_all | solution.py:41
  294.6 3.4 %bitcast_reduce_fusion = bf16[4,128,2560]{2,1,0:T(8,128)(2,1)S(1)} fusion(bf16[8,128,2560]{2,1,0:T(8,128)(2,1)} %all-to-all-done.1), kind=kLoop, calls=%fused_computation.3 | loop fusion | flops 1310720 | bytes 7864320 | tf_op jit(solution)/shard_map/reduce_sum | solution.py:43
  298.0 0.5 convolution_multiply_fusion
  298.5 1.4 fusion.7
  (19 shorter events, 0.3 us)
Async XLA Ops:
  6.5 3.8 %copy-start = (bf16[128,2560]{1,0:T(8,128)(2,1)S(1)}, bf16[128,2560]{1,0:T(8,128)(2,1)}, u32[]{:S(2)}) copy-start(bf16[128,2560]{1,0:T(8,128)(2,1)} %param.5) | copy-start | bytes 1966084
  6.5 159.1 %all-reduce.2.cloned.1.call-start = ((), (), s32[]{:S(2)}) async-start(), calls=%async_computation.2 | async-start | bytes 6291456 | tf_op jit(solution)/shard_map/psum | solution.py:9
  11.2 121.5 %slice-start = ((s8[7864320]{0:T(1024)(128)(4,1)}), s8[3670016]{0:T(1024)(128)(4,1)S(1)}, s32[]{:S(2)}) async-start(s8[7864320]{0:T(1024)(128)(4,1)} %bitcast.56), calls=%async_computation.3 | async-start | bytes 7340032
  11.7 121.1 %slice-start.1 = ((s8[7864320]{0:T(1024)(128)(4,1)}), s8[4194304]{0:T(1024)(128)(4,1)S(1)}, s32[]{:S(2)}) async-start(s8[7864320]{0:T(1024)(128)(4,1)} %bitcast.56), calls=%async_computation.4 | async-start | bytes 8388608
  165.6 3.1 copy-start.2
  174.8 6.2 %copy-start.1 = (f32[128,2]{0,1:T(2,128)S(1)}, f32[128,2]{0,1:T(2,128)}, u32[]{:S(2)}) copy-start(f32[128,2]{0,1:T(2,128)} %param.7) | copy-start | bytes 3076
  174.8 119.8 %all-to-all-start.1 = ((bf16[8,128,2560]{2,1,0:T(8,128)(2,1)}), bf16[8,128,2560]{2,1,0:T(8,128)(2,1)}, u32[]{:S(2)}, u32[]{:S(2)}) async-start(bf16[8,128,2560]{2,1,0:T(8,128)(2,1)} %bitcast.53), calls=%async_computation.1 | async-start | bytes 10485760 | tf_op jit(solution)/shard_map/all_to_all | solution.py:41
Sparse Core Ops, SparseCore 0:
  142.6 22.9 all-reduce.1
where the time goes:
time: 311 us; the launch traced here: 307 us
  waiting for transfers between devices  137 us (44%)
  blocking collectives  121 us (39%)
  matrix products  18.6 us (6%)
  between operations  13.5 us (4%)
  other arithmetic  8.6 us (3%)
  starting transfers between devices  6.19 us (2%)
    all_to_all x1, blocking collectives, per_device(): lax.all_to_all(outgoing, 'ctx', split_axis=0, concat_axis=0, tiled=True)  121 us
    all_to_all x1, waiting for transfers between devices, per_device(): lax.all_to_all(partial_out, 'ctx', split_axis=0, concat_axis=0, tiled=True)  113 us
    psum x1, waiting for transfers between devices, expert_half(): summed = lax.psum(gate_up.astype(jnp.bfloat16), 'exp').astype(jnp.float32)  23.2 us
    dot_general x1, matrix products, expert_half(): gate_up = jnp.dot(rows, w_in[0], preferred_element_type=jnp.float32)  9.68 us
  transfers between devices with their start and end apart: 2, of which 2 were waited for; matrix products, arithmetic and copies ran while one was open for 0% of the time, Pallas kernels for 0%

commit v1 on v0

--- a/solution.py
+++ b/solution.py
@@ -12,12 +12,28 @@
     return jnp.dot(hidden, w_out[0], preferred_element_type=jnp.float32).astype(jnp.bfloat16)
 
 
+def gate_table(route_ids, route_gates, experts):
+    named = route_ids[:, :, None] == jnp.arange(experts, dtype=jnp.int32)
+    return jnp.sum(jnp.where(named, route_gates[:, :, None], 0.0), axis=1)
+
+
+def dense(tokens, route_ids, route_gates, w_in, w_out):
+    experts = lax.axis_size("ctx") // 2
+    gates = lax.all_gather(gate_table(route_ids, route_gates, experts), "ctx", axis=0, tiled=True)
+    gate = lax.dynamic_slice_in_dim(gates, lax.axis_index("ctx") // 2, 1, axis=1)
+    rows = lax.all_gather(tokens, "ctx", axis=0, tiled=True)
+    out = (expert_half(rows, w_in, w_out).astype(jnp.float32) * gate).astype(jnp.bfloat16)
+    return lax.psum_scatter(out, "ctx", scatter_dimension=0, tiled=True)
+
+
 def per_device(tokens, route_ids, route_gates, w_in, w_out):
     ctx_size = lax.axis_size("ctx")
     experts = ctx_size // 2
     tok_rows, half_width = tokens.shape
     top_count = route_ids.shape[1]
     capacity = 2 * ((top_count * tok_rows + experts - 1) // experts)
+    if capacity >= tok_rows:
+        return dense(tokens, route_ids, route_gates, w_in, w_out)
     slots = experts * capacity
     flat_ids = route_ids.reshape(-1)
     onehot = (flat_ids[:, None] == jnp.arange(experts, dtype=jnp.int32)[None, :]).astype(jnp.int32)

time: 311 us -> 254 us (0.82)
  blocking collectives: 121 us -> 25.7 us
  waiting for transfers between devices: 137 us -> 191 us
  starting transfers between devices: 6.19 us -> 0.08 us
  other arithmetic: 8.6 us -> 2.91 us
    all_to_all x1 -> x0, blocking collectives: 121 us -> none  [per_device(): lax.all_to_all(outgoing, 'ctx', split_axis=0, concat_axis=0, tiled=True)]
    all_to_all x1 -> x0, waiting for transfers between devices: 113 us -> none  [per_device(): lax.all_to_all(partial_out, 'ctx', split_axis=0, concat_axis=0, tiled=True)]
    reduce_scatter x0 -> x1, waiting for transfers between devices: none -> 102 us  [dense(): return lax.psum_scatter(out, 'ctx', scatter_dimension=0, tiled=True)]
    all_gather x0 -> x1, waiting for transfers between devices: none -> 88.4 us  [dense(): rows = lax.all_gather(tokens, 'ctx', axis=0, tiled=True)]
    all_gather x0 -> x1, blocking collectives: none -> 25.7 us  [dense(): lax.all_gather(gate_table(route_ids, route_gates, experts), 'ctx', axis=0...]
    psum x1, waiting for transfers between devices: 23.2 us -> 0.02 us  [expert_half(): summed = lax.psum(gate_up.astype(jnp.bfloat16), 'exp').astype(jnp.float32)]
    all_to_all x1 -> x0, starting transfers between devices: 6.18 us -> none  [per_device(): lax.all_to_all(partial_out, 'ctx', split_axis=0, concat_axis=0, tiled=True)]
    dot_general x1, matrix products: 9.68 us -> 13.3 us  [expert_half(): gate_up = jnp.dot(rows, w_in[0], preferred_element_type=jnp.float32)]
  transfers between devices with their start and end apart: 2 -> 3, of which waited for: 2 -> 2; matrix products, arithmetic and copies ran while one was open for 0% -> 0% of each run, Pallas kernels for 0% -> 0%
where the time goes in v1:
time: 254 us; the launch traced here: 252 us
  waiting for transfers between devices  191 us (75%)
  blocking collectives  25.7 us (10%)
  matrix products  19.5 us (8%)
  between operations  13.2 us (5%)
  other arithmetic  2.91 us (1%)
    reduce_scatter x1, waiting for transfers between devices, dense(): return lax.psum_scatter(out, 'ctx', scatter_dimension=0, tiled=True)  102 us
    all_gather x1, waiting for transfers between devices, dense(): rows = lax.all_gather(tokens, 'ctx', axis=0, tiled=True)  88.4 us
    all_gather x1, blocking collectives, dense(): lax.all_gather(gate_table(route_ids, route_gates, experts), 'ctx', axis=0...  25.7 us
    dot_general x1, matrix products, expert_half(): gate_up = jnp.dot(rows, w_in[0], preferred_element_type=jnp.float32)  13.3 us
    dot_general x1, matrix products, expert_half(): jnp.dot(hidden, w_out[0], preferred_element_type=jnp.float32)  6.13 us
  transfers between devices with their start and end apart: 3, of which 2 were waited for; matrix products, arithmetic and copies ran while one was open for 0% of the time, Pallas kernels for 0%

profile of v1, /device:TPU:8, one launch (start us, length us, event | category | flops | bytes accessed | tf_op | source)
XLA Modules:
  0.0 252.4 jit_solution(14668510302520521451)
XLA Ops:
  6.5 0.0 all-gather.2.cloned.1.call-start
  6.5 0.7 all-gather.2.cloned.1.call-update
  7.3 0.0 copy-start
  7.3 0.0 copy-start.1
  7.3 0.0 all-reduce.2.cloned.1.call-start
  7.3 88.4 %all-gather.2.cloned.1.call-done = bf16[1024,2560]{1,0:T(8,128)(2,1)} async-done(((bf16[128,2560]{1,0:T(8,128)(2,1)}), bf16[1024,2560]{1,0:T(8,128)(2,1)}) %all-gather.2.cloned.1.call-update) | async-done | bytes 5242896 | tf_op jit(solution)/shard_map/all_gather | solution.py:24
  95.8 13.3 %fusion.3 = bf16[1024,1536]{1,0:T(8,128)(2,1)} fusion(bf16[1024,2560]{1,0:T(8,128)(2,1)} %all-gather.2.cloned.1.call-done, bf16[1,2560,1536]{2,1,0:T(8,128)(2,1)} %param.8), kind=kOutput, calls=%fused_computation.5 | convolution fusion | flops 8054636544 | bytes 16252928 | tf_op jit(solution)/shard_map/dot_general | solution.py:8
  109.1 0.0 all-reduce.2.cloned.1.call-update
  109.1 0.0 reduce-scatter.2.cloned.1.call-start
  109.2 0.0 copy-done
  109.2 0.0 copy-done.1
  109.2 25.7 %all_gather.7 = f32[1024,4]{0,1:T(4,128)S(1)} all-gather(f32[128,4]{0,1:T(4,128)S(1)} %select_reduce_fusion), channel_id=1, replica_groups=mesh['groups'=2,'ctx'=8,'exp'=2] {'ctx'}, dimensions={0}, use_global_device_ids=true | all-gather | bytes 18432 | tf_op jit(solution)/shard_map/all_gather | solution.py:22
  135.0 0.0 all-reduce.2.cloned.1.call-done
  135.0 0.0 copy-start.2
  135.0 2.9 %convert_element_type.19 = f32[1024,1536]{1,0:T(8,128)S(1)} convert(bf16[1024,1536]{1,0:T(8,128)(2,1)} %all-reduce.2.cloned.1.call-done) | non-fusion elementwise | flops 1572864 | bytes 9437184 | tf_op jit(solution)/shard_map/convert_element_type | solution.py:9
  137.9 0.1 copy-done.2
  138.0 6.1 %multiply_convert_fusion = bf16[1024,2560]{1,0:T(8,128)(2,1)} fusion(f32[1024]{0:T(1024)S(1)} %bitcast.10, bf16[1,768,2560]{2,1,0:T(8,128)(2,1)S(1)} %copy-done.2, f32[1024,1536]{1,0:T(8,128)S(1)} %convert_element_type.19), kind=kOutput, calls=%fused_computation | convolution fusion | flops 4041736192 | bytes 15470592 | tf_op jit(solution)/shard_map/dot_general | solution.py:12
  144.2 0.0 reduce-scatter.2.cloned.1.call-update
  144.2 101.7 %reduce-scatter.2.cloned.1.call-done = bf16[128,2560]{1,0:T(8,128)(2,1)} async-done(((bf16[1024,2560]{1,0:T(8,128)(2,1)}), bf16[128,2560]{1,0:T(8,128)(2,1)}) %reduce-scatter.2.cloned.1.call-update) | async-done | bytes 655376 | tf_op jit(solution)/shard_map/reduce_scatter | solution.py:26
  (2 shorter events, 0.0 us)
Async XLA Ops:
  6.5 89.2 %all-gather.2.cloned.1.call-start = ((), (), s32[]{:S(2)}) async-start(), calls=%async_computation.1 | async-start | bytes 5898240 | tf_op jit(solution)/shard_map/all_gather | solution.py:24
  7.3 101.9 %copy-start = (f32[128,2]{0,1:T(2,128)S(1)}, f32[128,2]{0,1:T(2,128)}, u32[]{:S(2)}) copy-start(f32[128,2]{0,1:T(2,128)} %param.7) | copy-start | bytes 3076
  7.3 101.9 %copy-start.1 = (s32[128,2]{0,1:T(2,128)S(1)}, s32[128,2]{0,1:T(2,128)}, u32[]{:S(2)}) copy-start(s32[128,2]{0,1:T(2,128)} %param.6) | copy-start | bytes 3076
  7.3 127.7 %all-reduce.2.cloned.1.call-start = ((), (), s32[]{:S(2)}) async-start(), calls=%async_computation.2 | async-start | bytes 6291456 | tf_op jit(solution)/shard_map/psum | solution.py:9
  109.1 136.7 %reduce-scatter.2.cloned.1.call-start = ((), (), s32[]{:S(2)}) async-start(), calls=%async_computation.3 | async-start | bytes 5898240 | tf_op jit(solution)/shard_map/reduce_scatter | solution.py:26
  135.0 3.1 %copy-start.2 = (bf16[1,768,2560]{2,1,0:T(8,128)(2,1)S(1)}, bf16[1,768,2560]{2,1,0:T(8,128)(2,1)}, u32[]{:S(2)}) copy-start(bf16[1,768,2560]{2,1,0:T(8,128)(2,1)} %param.9) | copy-start | bytes 11796484
Sparse Core Ops, SparseCore 0:
  9.5 86.1 all-gather.1
  109.2 22.5 all-reduce.1
  144.3 101.4 reduce-scatter.1

commit v2 on v0

--- a/solution.py
+++ b/solution.py
@@ -1,7 +1,248 @@
+import functools
+
 import jax
 import jax.numpy as jnp
 from jax import lax
+from jax.experimental import pallas as pl
+from jax.experimental.pallas import tpu as pltpu
 from jax.sharding import PartitionSpec as P
+
+MESH = pl.DeviceIdType.MESH
+
+
+def ordered(z, planes, step):
+    if step == 0:
+        return z
+    near = jnp.minimum(z, planes - 1 - z)
+    paired = jnp.where(step % 2 == 1, z - (step + 1) // 2, z + (step + 1) // 2)
+    rest = jnp.where(2 * z < planes - 1, z + step - near, z - step + near)
+    return jnp.where(step <= 2 * near, paired, rest)
+
+
+def layer_kernel(planes, tokens_hbm, gates_ref, w_in_hbm, w_out_hbm, mixed_ref,
+                 w_in, w_out, rows, gates, mine, theirs, hidden, halves, from_y, to_z, from_z,
+                 load_sem, gate_send, gate_recv, row_recv, up_send, down_send, y_send, mine_send, theirs_recv,
+                 back_send, back_recv, out_send, out_recv, core_sem):
+    ctx = 2 * planes
+    me = lax.axis_index("ctx")
+    core = lax.axis_index("exp")
+    z, y = me // 2, me % 2
+    side = z * 2 + 1 - y
+    count, width = tokens_hbm.shape
+    fh = w_out.shape[0]
+
+    load_rows = pltpu.make_async_copy(tokens_hbm, rows.at[z, y], load_sem.at[0])
+    load_in = pltpu.make_async_copy(w_in_hbm.at[0], w_in, load_sem.at[1])
+    load_out = pltpu.make_async_copy(w_out_hbm.at[0], w_out, load_sem.at[2])
+    load_gates = pltpu.make_async_copy(gates_ref, gates.at[me], load_sem.at[3])
+    load_rows.start()
+    load_gates.start()
+    load_in.start()
+    load_out.start()
+
+    barrier = pltpu.get_barrier_semaphore()
+    for step in range(1, ctx):
+        pl.semaphore_signal(barrier, inc=1, device_id={"ctx": (me + step) % ctx}, device_id_type=MESH)
+    pl.semaphore_signal(barrier, inc=1, device_id={"exp": 1 - core}, device_id_type=MESH)
+    pl.semaphore_wait(barrier, ctx)
+
+    def remote(src, dst, send, recv, **device):
+        return pltpu.make_async_remote_copy(
+            src_ref=src, dst_ref=dst, send_sem=send, recv_sem=recv, device_id=device, device_id_type=MESH)
+
+    def row_copy(plane, send, target):
+        return remote(rows.at[plane, y], rows.at[plane, y], send, row_recv.at[plane, y], ctx=target)
+
+    def gate_copy(step):
+        return remote(gates.at[me], gates.at[me], gate_send.at[step], gate_recv.at[me], ctx=(me + step) % ctx)
+
+    def hop(plane):
+        onward = jnp.where(plane < z, z + 1, z - 1)
+        return onward, jnp.logical_and(onward >= 0, onward < planes)
+
+    load_rows.wait()
+
+    up = row_copy(z, up_send.at[0], jnp.minimum(z + 1, planes - 1) * 2 + y)
+    down = row_copy(z, down_send.at[0], jnp.maximum(z - 1, 0) * 2 + y)
+
+    @pl.when(z + 1 < planes)
+    def _():
+        up.start()
+
+    @pl.when(z >= 1)
+    def _():
+        down.start()
+
+    row_copy(z, y_send.at[0], side).start()
+    load_gates.wait()
+    for step in range(1, ctx):
+        gate_copy(step).start()
+
+    def forward(step):
+        plane = ordered(z, planes, step)
+        row_copy(plane, y_send.at[step], side).wait_recv()
+        onward, there = hop(plane)
+
+        @pl.when(there)
+        def _():
+            row_copy(plane, up_send.at[step], jnp.clip(onward, 0, planes - 1) * 2 + y).start()
+
+        row_copy(plane, y_send.at[step], side).start()
+
+    def core_copy(step):
+        return remote(mine.at[step], theirs.at[step], mine_send.at[step], theirs_recv.at[step], exp=1 - core)
+
+    def first(step):
+        plane = ordered(z, planes, step)
+        remote(rows.at[plane, 1 - y], rows.at[plane, 1 - y], y_send.at[step], row_recv.at[plane, 1 - y],
+               ctx=side).wait_recv()
+
+        @pl.loop(0, 2 * fh // TILE)
+        def _(tile):
+            columns = pl.ds(pl.multiple_of(tile * TILE, TILE), TILE)
+            mine[step, :, columns] = jnp.dot(
+                rows[plane].reshape(2 * count, width), w_in[:, columns], preferred_element_type=jnp.float32
+            ).astype(jnp.bfloat16)
+
+        core_copy(step).start()
+
+    def gate_column(block):
+        line = gates[block, pl.ds(z, 1), :]
+        shape = (count, count)
+        diagonal = lax.broadcasted_iota(jnp.int32, shape, 0) == lax.broadcasted_iota(jnp.int32, shape, 1)
+        return jnp.sum(jnp.where(diagonal, jnp.broadcast_to(line, shape), 0.0), axis=1, keepdims=True)
+
+    def second(step):
+        plane = ordered(z, planes, step)
+        core_copy(step).wait_recv()
+        gate = mine[step, :, :fh].astype(jnp.float32) + theirs[step, :, :fh].astype(jnp.float32)
+        up_value = mine[step, :, fh:].astype(jnp.float32) + theirs[step, :, fh:].astype(jnp.float32)
+        hidden[...] = (jax.nn.silu(gate) * up_value).astype(jnp.bfloat16)
+        scale = jnp.concatenate([gate_column(plane * 2), gate_column(plane * 2 + 1)], axis=0)
+
+        @pl.loop(0, width // TILE)
+        def _(tile):
+            columns = pl.ds(pl.multiple_of(tile * TILE, TILE), TILE)
+            out = jnp.dot(hidden[...], w_out[:, columns], preferred_element_type=jnp.float32) * scale
+            halves[plane, :, :, columns] = out.astype(jnp.bfloat16).reshape(2, count, TILE)
+
+    def back_copy(step):
+        plane = ordered(z, planes, step)
+        return remote(halves.at[plane, 1 - y], from_y.at[plane], back_send.at[step], back_recv.at[plane], ctx=side)
+
+    def out_copy(step):
+        plane = ordered(z, planes, step)
+        return remote(to_z.at[step], from_z.at[z], out_send.at[step], out_recv.at[z], ctx=plane * 2 + y)
+
+    def reduce(step):
+        plane = ordered(z, planes, step)
+        back_copy(step).wait_recv()
+        to_z[step] = (halves[plane, y].astype(jnp.float32) + from_y[plane].astype(jnp.float32)).astype(jnp.bfloat16)
+        out_copy(step).start()
+
+    for step in range(planes):
+        if step + 1 < planes:
+            forward(step + 1)
+        if step == 0:
+            load_in.wait()
+        first(step)
+        if step == 0:
+            load_out.wait()
+            for other in range(1, ctx):
+                source = (me + other) % ctx
+                remote(gates.at[source], gates.at[source], gate_send.at[other], gate_recv.at[source],
+                       ctx=source).wait_recv()
+        if step >= 1:
+            second(step - 1)
+            if step >= 2:
+                back_copy(step - 1).start()
+    second(planes - 1)
+    if planes > 1:
+        back_copy(planes - 1).start()
+    back_copy(0).start()
+    for step in range(1, planes):
+        reduce(step)
+    back_copy(0).wait_recv()
+    for step in range(1, planes):
+        plane = ordered(z, planes, step)
+        remote(to_z.at[step], from_z.at[plane], out_send.at[step], out_recv.at[plane], ctx=plane * 2 + y).wait_recv()
+
+    @pl.loop(0, width // TILE)
+    def _(tile):
+        columns = pl.ds(pl.multiple_of(tile * TILE, TILE), TILE)
+        total = halves[z, y, :, columns].astype(jnp.float32) + from_y[z, :, columns].astype(jnp.float32)
+        for step in range(1, planes):
+            total = total + from_z[ordered(z, planes, step), :, columns].astype(jnp.float32)
+        mixed_ref[:, columns] = total.astype(jnp.bfloat16)
+
+    @pl.when(z + 1 < planes)
+    def _():
+        up.wait_send()
+
+    @pl.when(z >= 1)
+    def _():
+        down.wait_send()
+
+    for step in range(planes):
+        plane = ordered(z, planes, step)
+        row_copy(plane, y_send.at[step], side).wait_send()
+        core_copy(step).wait_send()
+        back_copy(step).wait_send()
+        if step:
+            out_copy(step).wait_send()
+            onward, there = hop(plane)
+
+            @pl.when(there)
+            def _():
+                row_copy(plane, up_send.at[step], jnp.clip(onward, 0, planes - 1) * 2 + y).wait_send()
+
+    for step in range(1, ctx):
+        gate_copy(step).wait_send()
+
+
+def gate_table(route_ids, route_gates, experts):
+    lines = -(-experts // 8) * 8
+    named = route_ids.T[:, None, :] == jnp.arange(lines, dtype=jnp.int32)[None, :, None]
+    return jnp.sum(jnp.where(named, route_gates.T[:, None, :], 0.0), axis=0)
+
+
+def dense(tokens, route_ids, route_gates, w_in, w_out):
+    ctx = lax.axis_size("ctx")
+    planes = ctx // 2
+    count, width = tokens.shape
+    fh = w_out.shape[1]
+    gates = gate_table(route_ids, route_gates, planes)
+    dma = pltpu.SemaphoreType.DMA
+    bf16 = jnp.bfloat16
+    hbm = pl.BlockSpec(memory_space=pl.ANY)
+    return pl.pallas_call(
+        functools.partial(layer_kernel, planes),
+        out_shape=jax.ShapeDtypeStruct((count, width), bf16),
+        in_specs=[hbm, pl.BlockSpec(memory_space=pltpu.VMEM), hbm, hbm],
+        out_specs=pl.BlockSpec(memory_space=pltpu.VMEM),
+        scratch_shapes=[
+            pltpu.VMEM(w_in.shape[1:], bf16),
+            pltpu.VMEM(w_out.shape[1:], bf16),
+            pltpu.VMEM((planes, 2, count, width), bf16),
+            pltpu.VMEM((ctx,) + gates.shape, jnp.float32),
+            pltpu.VMEM((planes, 2 * count, 2 * fh), bf16),
+            pltpu.VMEM((planes, 2 * count, 2 * fh), bf16),
+            pltpu.VMEM((2 * count, fh), bf16),
+            pltpu.VMEM((planes, 2, count, width), bf16),
+            pltpu.VMEM((planes, count, width), bf16),
+            pltpu.VMEM((planes, count, width), bf16),
+            pltpu.VMEM((planes, count, width), bf16),
+            dma((4,)), dma((ctx,)), dma((ctx,)), dma((planes, 2)),
+            dma((planes,)), dma((1,)), dma((planes,)), dma((planes,)), dma((planes,)),
+            dma((planes,)), dma((planes,)), dma((planes,)), dma((planes,)), dma((1,)),
+        ],
+        compiler_params=pltpu.CompilerParams(
+            collective_id=0, has_side_effects=True, vmem_limit_bytes=60 * 1024 * 1024),
+        name="experts",
+    )(tokens, gates, w_in, w_out)
+
+
+TILE = 256
 
 
 def expert_half(rows, w_in, w_out):
@@ -18,6 +259,8 @@
     tok_rows, half_width = tokens.shape
     top_count = route_ids.shape[1]
     capacity = 2 * ((top_count * tok_rows + experts - 1) // experts)
+    if capacity >= tok_rows:
+        return dense(tokens, route_ids, route_gates, w_in, w_out)
     slots = experts * capacity
     flat_ids = route_ids.reshape(-1)
     onehot = (flat_ids[:, None] == jnp.arange(experts, dtype=jnp.int32)[None, :]).astype(jnp.int32)

time: 311 us -> 152 us (0.49)
  Pallas kernels: 0 us -> 147 us
  waiting for transfers between devices: 137 us -> 0 us
  blocking collectives: 121 us -> 0 us
  matrix products: 18.6 us -> 0 us
  between operations: 13.5 us -> 0.01 us
  other arithmetic: 8.6 us -> 1.29 us
  starting transfers between devices: 6.19 us -> 0 us
    pallas_call x0 -> x1, Pallas kernels: none -> 147 us  [dense(): pl.pallas_call(functools.partial(layer_kernel, planes), out_shape=jax.Sha...]
    all_to_all x1 -> x0, blocking collectives: 121 us -> none  [per_device(): lax.all_to_all(outgoing, 'ctx', split_axis=0, concat_axis=0, tiled=True)]
    all_to_all x1 -> x0, waiting for transfers between devices: 113 us -> none  [per_device(): lax.all_to_all(partial_out, 'ctx', split_axis=0, concat_axis=0, tiled=True)]
    psum x1 -> x0, waiting for transfers between devices: 23.2 us -> none  [expert_half(): summed = lax.psum(gate_up.astype(jnp.bfloat16), 'exp').astype(jnp.float32)]
    dot_general x5 -> x0, matrix products: 18.6 us -> none  [the longest x1 9.68 us: expert_half(): gate_up = jnp.dot(rows, w_in[0], preferred_element_type=jnp.float32)]
    all_to_all x1 -> x0, starting transfers between devices: 6.18 us -> none  [per_device(): lax.all_to_all(partial_out, 'ctx', split_axis=0, concat_axis=0, tiled=True)]
  transfers between devices with their start and end apart: 2 -> 0, of which waited for: 2 -> 0; matrix products, arithmetic and copies ran while one was open for 0% -> 0% of each run, Pallas kernels for 0% -> 0%
where the time goes in v2:
time: 152 us; the launch traced here: 150 us
  Pallas kernels  147 us (97%)
  local copies, waits for them, and re-layouts  1.97 us (1%)
    pallas_call x1, Pallas kernels, dense(): pl.pallas_call(functools.partial(layer_kernel, planes), out_shape=jax.Sha...  147 us

profile of v2, /device:TPU:8, one launch (start us, length us, event | category | flops | bytes accessed | tf_op | source)
XLA Modules:
  0.0 150.3 jit_solution(10488209576363404921)
XLA Ops:
  0.0 1.3 select_reduce_fusion.gates_ref
  1.3 147.0 %experts.1 = bf16[128,2560]{1,0:T(8,128)(2,1)} custom-call(bf16[128,2560]{1,0:T(8,128)(2,1)} %tokens_hbm.1, f32[8,128]{1,0:T(8,128)} %select_reduce_fusion.gates_ref, bf16[1,2560,1536]{2,1,0:T(8,128)(2,1)} %w_in_hbm.1, bf16[1,768,2560]{2,1,0:T(8,128)(2,1)} %w_out_hbm.1), custom_call_target="tpu_custom_call" | custom-call | tf_op jit(solution)/shard_map/experts/pallas_call | solution.py:218
  148.3 2.0 %copy.7 = bf16[128,2560]{1,0:T(8,128)(2,1)} copy(bf16[128,2560]{1,0:T(8,128)(2,1)} %experts.1) | data formatting | bytes 1310720

commit v3 on v2

--- a/solution.py
+++ b/solution.py
@@ -20,9 +20,9 @@
 
 
 def layer_kernel(planes, tokens_hbm, gates_ref, w_in_hbm, w_out_hbm, mixed_ref,
-                 w_in, w_out, rows, gates, mine, theirs, hidden, halves, from_y, to_z, from_z,
+                 w_in, w_out, rows, gates, mine, theirs, hidden, halves, from_y, to_z, from_z, total,
                  load_sem, gate_send, gate_recv, row_recv, up_send, down_send, y_send, mine_send, theirs_recv,
-                 back_send, back_recv, out_send, out_recv, core_sem):
+                 back_send, back_recv, out_send, out_recv):
     ctx = 2 * planes
     me = lax.axis_index("ctx")
     core = lax.axis_index("exp")
@@ -30,6 +30,7 @@
     side = z * 2 + 1 - y
     count, width = tokens_hbm.shape
     fh = w_out.shape[0]
+    chunks, span = to_z.shape[1], to_z.shape[3]
 
     load_rows = pltpu.make_async_copy(tokens_hbm, rows.at[z, y], load_sem.at[0])
     load_in = pltpu.make_async_copy(w_in_hbm.at[0], w_in, load_sem.at[1])
@@ -103,8 +104,9 @@
             mine[step, :, columns] = jnp.dot(
                 rows[plane].reshape(2 * count, width), w_in[:, columns], preferred_element_type=jnp.float32
             ).astype(jnp.bfloat16)
-
-        core_copy(step).start()
+            remote(mine.at[step, :, columns], theirs.at[step, :, columns], mine_send.at[step], theirs_recv.at[step],
+                   exp=1 - core).start()
+
 
     def gate_column(block):
         line = gates[block, pl.ds(z, 1), :]
@@ -112,7 +114,7 @@
         diagonal = lax.broadcasted_iota(jnp.int32, shape, 0) == lax.broadcasted_iota(jnp.int32, shape, 1)
         return jnp.sum(jnp.where(diagonal, jnp.broadcast_to(line, shape), 0.0), axis=1, keepdims=True)
 
-    def second(step):
+    def second(step, sends):
         plane = ordered(z, planes, step)
         core_copy(step).wait_recv()
         gate = mine[step, :, :fh].astype(jnp.float32) + theirs[step, :, :fh].astype(jnp.float32)
@@ -120,25 +122,51 @@
         hidden[...] = (jax.nn.silu(gate) * up_value).astype(jnp.bfloat16)
         scale = jnp.concatenate([gate_column(plane * 2), gate_column(plane * 2 + 1)], axis=0)
 
-        @pl.loop(0, width // TILE)
-        def _(tile):
-            columns = pl.ds(pl.multiple_of(tile * TILE, TILE), TILE)
-            out = jnp.dot(hidden[...], w_out[:, columns], preferred_element_type=jnp.float32) * scale
-            halves[plane, :, :, columns] = out.astype(jnp.bfloat16).reshape(2, count, TILE)
-
-    def back_copy(step):
-        plane = ordered(z, planes, step)
-        return remote(halves.at[plane, 1 - y], from_y.at[plane], back_send.at[step], back_recv.at[plane], ctx=side)
-
-    def out_copy(step):
-        plane = ordered(z, planes, step)
-        return remote(to_z.at[step], from_z.at[z], out_send.at[step], out_recv.at[z], ctx=plane * 2 + y)
+        @pl.loop(0, chunks)
+        def _(chunk):
+            for at in range(0, span, TILE):
+                columns = pl.ds(pl.multiple_of(chunk * span + at, TILE), TILE)
+                out = jnp.dot(hidden[...], w_out[:, columns], preferred_element_type=jnp.float32) * scale
+                halves[plane, :, chunk, :, at:at + TILE] = out.astype(jnp.bfloat16).reshape(2, count, TILE)
+            if sends:
+                back_copy(step, chunk).start()
+
+    def back_copy(step, chunk):
+        plane = ordered(z, planes, step)
+        return remote(halves.at[plane, 1 - y, chunk], from_y.at[plane, chunk], back_send.at[step, chunk],
+                      back_recv.at[plane, chunk], ctx=side)
+
+    def out_copy(step, chunk):
+        plane = ordered(z, planes, step)
+        onward = jnp.where(plane > z, z + 1, z - 1)
+        slot = jnp.where(jnp.logical_and(onward == plane, plane < z), planes, plane)
+        return remote(to_z.at[step, chunk], from_z.at[slot, chunk], out_send.at[step, chunk],
+                      out_recv.at[slot, chunk], ctx=onward * 2 + y)
+
+    def wait_chain(slot, chunk):
+        remote(to_z.at[0, chunk], from_z.at[slot, chunk], out_send.at[0, chunk], out_recv.at[slot, chunk],
+               ctx=side).wait_recv()
 
     def reduce(step):
         plane = ordered(z, planes, step)
-        back_copy(step).wait_recv()
-        to_z[step] = (halves[plane, y].astype(jnp.float32) + from_y[plane].astype(jnp.float32)).astype(jnp.bfloat16)
-        out_copy(step).start()
+        passes = jnp.where(plane > z, z >= 1, z + 1 < planes)
+
+        @pl.loop(0, chunks)
+        def _(chunk):
+            back_copy(step, chunk).wait_recv()
+
+            @pl.when(passes)
+            def _():
+                wait_chain(plane, chunk)
+                value = halves[plane, y, chunk].astype(jnp.float32) + from_y[plane, chunk].astype(jnp.float32)
+                to_z[step, chunk] = (value + from_z[plane, chunk].astype(jnp.float32)).astype(jnp.bfloat16)
+
+            @pl.when(jnp.logical_not(passes))
+            def _():
+                value = halves[plane, y, chunk].astype(jnp.float32) + from_y[plane, chunk].astype(jnp.float32)
+                to_z[step, chunk] = value.astype(jnp.bfloat16)
+
+            out_copy(step, chunk).start()
 
     for step in range(planes):
         if step + 1 < planes:
@@ -152,28 +180,36 @@
                 source = (me + other) % ctx
                 remote(gates.at[source], gates.at[source], gate_send.at[other], gate_recv.at[source],
                        ctx=source).wait_recv()
-        if step >= 1:
-            second(step - 1)
-            if step >= 2:
-                back_copy(step - 1).start()
-    second(planes - 1)
-    if planes > 1:
-        back_copy(planes - 1).start()
-    back_copy(0).start()
-    for step in range(1, planes):
+        if 1 <= step < planes - 1:
+            second(step - 1, False)
+        if step == planes - 2:
+            second(step, step >= 1)
+    second(planes - 1, planes > 1)
+
+    for step in list(range(planes - 3, 0, -1)) + [0]:
+        @pl.loop(0, chunks)
+        def _(chunk):
+            back_copy(step, chunk).start()
+
+    for step in [planes - 2] * (planes > 2) + [planes - 1] * (planes > 1) + list(range(planes - 3, 0, -1)):
         reduce(step)
-    back_copy(0).wait_recv()
-    for step in range(1, planes):
-        plane = ordered(z, planes, step)
-        remote(to_z.at[step], from_z.at[plane], out_send.at[step], out_recv.at[plane], ctx=plane * 2 + y).wait_recv()
-
-    @pl.loop(0, width // TILE)
-    def _(tile):
-        columns = pl.ds(pl.multiple_of(tile * TILE, TILE), TILE)
-        total = halves[z, y, :, columns].astype(jnp.float32) + from_y[z, :, columns].astype(jnp.float32)
-        for step in range(1, planes):
-            total = total + from_z[ordered(z, planes, step), :, columns].astype(jnp.float32)
-        mixed_ref[:, columns] = total.astype(jnp.bfloat16)
+
+    @pl.loop(0, chunks)
+    def _(chunk):
+        back_copy(0, chunk).wait_recv()
+        total[...] = halves[z, y, chunk].astype(jnp.float32) + from_y[z, chunk].astype(jnp.float32)
+
+        @pl.when(z >= 1)
+        def _():
+            wait_chain(z, chunk)
+            total[...] += from_z[z, chunk].astype(jnp.float32)
+
+        @pl.when(z + 1 < planes)
+        def _():
+            wait_chain(planes, chunk)
+            total[...] += from_z[planes, chunk].astype(jnp.float32)
+
+        mixed_ref[:, pl.ds(pl.multiple_of(chunk * span, span), span)] = total[...].astype(jnp.bfloat16)
 
     @pl.when(z + 1 < planes)
     def _():
@@ -187,9 +223,11 @@
         plane = ordered(z, planes, step)
         row_copy(plane, y_send.at[step], side).wait_send()
         core_copy(step).wait_send()
-        back_copy(step).wait_send()
+        for chunk in range(chunks):
+            back_copy(step, chunk).wait_send()
         if step:
-            out_copy(step).wait_send()
+            for chunk in range(chunks):
+                out_copy(step, chunk).wait_send()
             onward, there = hop(plane)
 
             @pl.when(there)
@@ -211,6 +249,8 @@
     planes = ctx // 2
     count, width = tokens.shape
     fh = w_out.shape[1]
+    span = SPAN if width % SPAN == 0 else width
+    chunks = width // span
     gates = gate_table(route_ids, route_gates, planes)
     dma = pltpu.SemaphoreType.DMA
     bf16 = jnp.bfloat16
@@ -228,13 +268,14 @@
             pltpu.VMEM((planes, 2 * count, 2 * fh), bf16),
             pltpu.VMEM((planes, 2 * count, 2 * fh), bf16),
             pltpu.VMEM((2 * count, fh), bf16),
-            pltpu.VMEM((planes, 2, count, width), bf16),
-            pltpu.VMEM((planes, count, width), bf16),
-            pltpu.VMEM((planes, count, width), bf16),
-            pltpu.VMEM((planes, count, width), bf16),
+            pltpu.VMEM((planes, 2, chunks, count, span), bf16),
+            pltpu.VMEM((planes, chunks, count, span), bf16),
+            pltpu.VMEM((planes, chunks, count, span), bf16),
+            pltpu.VMEM((planes + 1, chunks, count, span), bf16),
+            pltpu.VMEM((count, span), jnp.float32),
             dma((4,)), dma((ctx,)), dma((ctx,)), dma((planes, 2)),
             dma((planes,)), dma((1,)), dma((planes,)), dma((planes,)), dma((planes,)),
-            dma((planes,)), dma((planes,)), dma((planes,)), dma((planes,)), dma((1,)),
+            dma((planes, chunks)), dma((planes, chunks)), dma((planes, chunks)), dma((planes + 1, chunks)),
         ],
         compiler_params=pltpu.CompilerParams(
             collective_id=0, has_side_effects=True, vmem_limit_bytes=60 * 1024 * 1024),
@@ -243,6 +284,7 @@
 
 
 TILE = 256
+SPAN = 512
 
 
 def expert_half(rows, w_in, w_out):

time: 152 us -> 147 us (0.967)
  Pallas kernels: 147 us -> 143 us
    pallas_call x1, Pallas kernels: 147 us -> 143 us  [dense(): pl.pallas_call(functools.partial(layer_kernel, planes), out_shape=jax.Sha...]
where the time goes in v3:
time: 147 us
  Pallas kernels  143 us (97%)
  local copies, waits for them, and re-layouts  1.97 us (1%)
    pallas_call x1, Pallas kernels, dense(): pl.pallas_call(functools.partial(layer_kernel, planes), out_shape=jax.Sha...  143 us

profile of v3, /device:TPU:8, one launch (start us, length us, event | category | flops | bytes accessed | tf_op | source)
XLA Modules:
  0.0 146.6 jit_solution(17218858659080240123)
XLA Ops:
  0.0 1.3 select_reduce_fusion.gates_ref
  1.3 143.3 %experts.1 = bf16[128,2560]{1,0:T(8,128)(2,1)} custom-call(bf16[128,2560]{1,0:T(8,128)(2,1)} %tokens_hbm.1, f32[8,128]{1,0:T(8,128)} %select_reduce_fusion.gates_ref, bf16[1,2560,1536]{2,1,0:T(8,128)(2,1)} %w_in_hbm.1, bf16[1,768,2560]{2,1,0:T(8,128)(2,1)} %w_out_hbm.1), custom_call_target="tpu_custom_call" | custom-call | tf_op jit(solution)/shard_map/experts/pallas_call | solution.py:258
  144.6 2.0 %copy.7 = bf16[128,2560]{1,0:T(8,128)(2,1)} copy(bf16[128,2560]{1,0:T(8,128)(2,1)} %experts.1) | data formatting | bytes 1310720

commit v4 on v3

--- a/solution.py
+++ b/solution.py
@@ -20,9 +20,9 @@
 
 
 def layer_kernel(planes, tokens_hbm, gates_ref, w_in_hbm, w_out_hbm, mixed_ref,
-                 w_in, w_out, rows, gates, mine, theirs, hidden, halves, from_y, to_z, from_z, total,
-                 load_sem, gate_send, gate_recv, row_recv, up_send, down_send, y_send, mine_send, theirs_recv,
-                 back_send, back_recv, out_send, out_recv):
+                 w_in, w_out, rows, gates, mine, theirs, hidden, halves, from_y, to_z, from_z, total, rest,
+                 load_sem, gate_send, gate_recv, row_recv, up_send, down_send, relay_send, y_send, mine_send, theirs_recv,
+                 back_send, back_recv, out_send, out_recv, rest_send, rest_recv):
     ctx = 2 * planes
     me = lax.axis_index("ctx")
     core = lax.axis_index("exp")
@@ -31,6 +31,9 @@
     count, width = tokens_hbm.shape
     fh = w_out.shape[0]
     chunks, span = to_z.shape[1], to_z.shape[3]
+    most = count - rest.shape[1]
+    pieces = row_recv.shape[2]
+    depth = count // pieces
 
     load_rows = pltpu.make_async_copy(tokens_hbm, rows.at[z, y], load_sem.at[0])
     load_in = pltpu.make_async_copy(w_in_hbm.at[0], w_in, load_sem.at[1])
@@ -51,8 +54,12 @@
         return pltpu.make_async_remote_copy(
             src_ref=src, dst_ref=dst, send_sem=send, recv_sem=recv, device_id=device, device_id_type=MESH)
 
-    def row_copy(plane, send, target):
-        return remote(rows.at[plane, y], rows.at[plane, y], send, row_recv.at[plane, y], ctx=target)
+    def row_copy(plane, column, piece, send, target):
+        part = rows.at[plane, column, pl.ds(piece * depth, depth)]
+        return remote(part, part, send, row_recv.at[plane, column, piece], ctx=target)
+
+    def wait_rows(plane, column, piece):
+        row_copy(plane, column, piece, y_send.at[0, 0], side).wait_recv()
 
     def gate_copy(step):
         return remote(gates.at[me], gates.at[me], gate_send.at[step], gate_recv.at[me], ctx=(me + step) % ctx)
@@ -63,40 +70,56 @@
 
     load_rows.wait()
 
-    up = row_copy(z, up_send.at[0], jnp.minimum(z + 1, planes - 1) * 2 + y)
-    down = row_copy(z, down_send.at[0], jnp.maximum(z - 1, 0) * 2 + y)
-
-    @pl.when(z + 1 < planes)
-    def _():
-        up.start()
-
-    @pl.when(z >= 1)
-    def _():
-        down.start()
-
-    row_copy(z, y_send.at[0], side).start()
+    above, below = jnp.minimum(z + 1, planes - 1) * 2 + y, jnp.maximum(z - 1, 0) * 2 + y
+
+    def spread(column, piece, act):
+        @pl.when(z + 1 < planes)
+        def _():
+            act(row_copy(z, column, piece, up_send.at[column, piece], above))
+
+        @pl.when(z >= 1)
+        def _():
+            act(row_copy(z, column, piece, down_send.at[column, piece], below))
+
+    for piece in range(pieces):
+        spread(y, piece, lambda copy: copy.start())
+        row_copy(z, y, piece, y_send.at[0, piece], side).start()
     load_gates.wait()
     for step in range(1, ctx):
         gate_copy(step).start()
 
-    def forward(step):
-        plane = ordered(z, planes, step)
-        row_copy(plane, y_send.at[step], side).wait_recv()
+    def relay(step, column, piece, act):
+        plane = ordered(z, planes, step)
         onward, there = hop(plane)
 
         @pl.when(there)
         def _():
-            row_copy(plane, up_send.at[step], jnp.clip(onward, 0, planes - 1) * 2 + y).start()
-
-        row_copy(plane, y_send.at[step], side).start()
+            act(row_copy(plane, column, piece, relay_send.at[step, column, piece],
+                         jnp.clip(onward, 0, planes - 1) * 2 + y))
+
+    def forward(step):
+        plane = ordered(z, planes, step)
+        for piece in range(pieces):
+            wait_rows(plane, y, piece)
+            relay(step, y, piece, lambda copy: copy.start())
+            if piece < pieces - 1:
+                row_copy(plane, y, piece, y_send.at[step, piece], side).start()
+
+    def crossed(step):
+        plane = ordered(z, planes, step)
+        wait_rows(plane, 1 - y, pieces - 1)
+        if step == 0:
+            spread(1 - y, pieces - 1, lambda copy: copy.start())
+        else:
+            relay(step, 1 - y, pieces - 1, lambda copy: copy.start())
 
     def core_copy(step):
         return remote(mine.at[step], theirs.at[step], mine_send.at[step], theirs_recv.at[step], exp=1 - core)
 
     def first(step):
         plane = ordered(z, planes, step)
-        remote(rows.at[plane, 1 - y], rows.at[plane, 1 - y], y_send.at[step], row_recv.at[plane, 1 - y],
-               ctx=side).wait_recv()
+        for piece in range(pieces - 1):
+            wait_rows(plane, 1 - y, piece)
 
         @pl.loop(0, 2 * fh // TILE)
         def _(tile):
@@ -133,7 +156,8 @@
 
     def back_copy(step, chunk):
         plane = ordered(z, planes, step)
-        return remote(halves.at[plane, 1 - y, chunk], from_y.at[plane, chunk], back_send.at[step, chunk],
+        part = pl.ds(0, most)
+        return remote(halves.at[plane, 1 - y, chunk, part], from_y.at[plane, chunk, part], back_send.at[step, chunk],
                       back_recv.at[plane, chunk], ctx=side)
 
     def out_copy(step, chunk):
@@ -158,17 +182,29 @@
             @pl.when(passes)
             def _():
                 wait_chain(plane, chunk)
-                value = halves[plane, y, chunk].astype(jnp.float32) + from_y[plane, chunk].astype(jnp.float32)
-                to_z[step, chunk] = (value + from_z[plane, chunk].astype(jnp.float32)).astype(jnp.bfloat16)
-
-            @pl.when(jnp.logical_not(passes))
-            def _():
-                value = halves[plane, y, chunk].astype(jnp.float32) + from_y[plane, chunk].astype(jnp.float32)
-                to_z[step, chunk] = value.astype(jnp.bfloat16)
-
+
+            def put(first, last, value):
+                @pl.when(passes)
+                def _():
+                    chained = value + from_z[plane, chunk, first:last].astype(jnp.float32)
+                    to_z[step, chunk, first:last] = chained.astype(jnp.bfloat16)
+
+                @pl.when(jnp.logical_not(passes))
+                def _():
+                    to_z[step, chunk, first:last] = value.astype(jnp.bfloat16)
+
+            own = halves[plane, y, chunk].astype(jnp.float32)
+            put(0, most, own[:most] + from_y[plane, chunk, :most].astype(jnp.float32))
+            put(most, count, own[most:])
+            put(count, 2 * count - most, halves[plane, 1 - y, chunk, most:].astype(jnp.float32))
             out_copy(step, chunk).start()
 
+    def rest_copy(chunk):
+        return remote(rest.at[chunk], from_y.at[z, chunk, pl.ds(most, count - most)], rest_send.at[chunk],
+                      rest_recv.at[chunk], ctx=side)
+
     for step in range(planes):
+        crossed(step)
         if step + 1 < planes:
             forward(step + 1)
         if step == 0:
@@ -194,45 +230,51 @@
     for step in [planes - 2] * (planes > 2) + [planes - 1] * (planes > 1) + list(range(planes - 3, 0, -1)):
         reduce(step)
 
+    def chains(first, last, chunk, act):
+        @pl.when(z >= 1)
+        def _():
+            act(z)
+            total[first:last] += from_z[z, chunk, first:last].astype(jnp.float32)
+
+        @pl.when(z + 1 < planes)
+        def _():
+            act(planes)
+            total[first:last] += from_z[planes, chunk, first:last].astype(jnp.float32)
+
+    @pl.loop(0, chunks)
+    def _(chunk):
+        total[count:] = halves[z, 1 - y, chunk, most:].astype(jnp.float32)
+        chains(count, 2 * count - most, chunk, lambda slot: wait_chain(slot, chunk))
+        rest[chunk] = total[count:].astype(jnp.bfloat16)
+        rest_copy(chunk).start()
+
     @pl.loop(0, chunks)
     def _(chunk):
         back_copy(0, chunk).wait_recv()
-        total[...] = halves[z, y, chunk].astype(jnp.float32) + from_y[z, chunk].astype(jnp.float32)
-
-        @pl.when(z >= 1)
-        def _():
-            wait_chain(z, chunk)
-            total[...] += from_z[z, chunk].astype(jnp.float32)
-
-        @pl.when(z + 1 < planes)
-        def _():
-            wait_chain(planes, chunk)
-            total[...] += from_z[planes, chunk].astype(jnp.float32)
-
-        mixed_ref[:, pl.ds(pl.multiple_of(chunk * span, span), span)] = total[...].astype(jnp.bfloat16)
-
-    @pl.when(z + 1 < planes)
-    def _():
-        up.wait_send()
-
-    @pl.when(z >= 1)
-    def _():
-        down.wait_send()
-
+        rest_copy(chunk).wait_recv()
+        total[:count] = halves[z, y, chunk].astype(jnp.float32) + from_y[z, chunk].astype(jnp.float32)
+        chains(0, count, chunk, lambda slot: None)
+        mixed_ref[:, pl.ds(pl.multiple_of(chunk * span, span), span)] = total[:count].astype(jnp.bfloat16)
+
+    finish = lambda copy: copy.wait_send()
+    for piece in range(pieces):
+        spread(y, piece, finish)
+    spread(1 - y, pieces - 1, finish)
+    for chunk in range(chunks):
+        rest_copy(chunk).wait_send()
     for step in range(planes):
         plane = ordered(z, planes, step)
-        row_copy(plane, y_send.at[step], side).wait_send()
+        for piece in range(pieces - (step > 0)):
+            row_copy(plane, y, piece, y_send.at[step, piece], side).wait_send()
         core_copy(step).wait_send()
         for chunk in range(chunks):
             back_copy(step, chunk).wait_send()
         if step:
             for chunk in range(chunks):
                 out_copy(step, chunk).wait_send()
-            onward, there = hop(plane)
-
-            @pl.when(there)
-            def _():
-                row_copy(plane, up_send.at[step], jnp.clip(onward, 0, planes - 1) * 2 + y).wait_send()
+            for piece in range(pieces):
+                relay(step, y, piece, finish)
+            relay(step, 1 - y, pieces - 1, finish)
 
     for step in range(1, ctx):
         gate_copy(step).wait_send()
@@ -251,6 +293,8 @@
     fh = w_out.shape[1]
     span = SPAN if width % SPAN == 0 else width
     chunks = width // span
+    pieces = PIECES if count % (16 * PIECES) == 0 else 1
+    late = max(16, count * LATE // 128 // 16 * 16)
     gates = gate_table(route_ids, route_gates, planes)
     dma = pltpu.SemaphoreType.DMA
     bf16 = jnp.bfloat16
@@ -270,12 +314,14 @@
             pltpu.VMEM((2 * count, fh), bf16),
             pltpu.VMEM((planes, 2, chunks, count, span), bf16),
             pltpu.VMEM((planes, chunks, count, span), bf16),
-            pltpu.VMEM((planes, chunks, count, span), bf16),
-            pltpu.VMEM((planes + 1, chunks, count, span), bf16),
-            pltpu.VMEM((count, span), jnp.float32),
-            dma((4,)), dma((ctx,)), dma((ctx,)), dma((planes, 2)),
-            dma((planes,)), dma((1,)), dma((planes,)), dma((planes,)), dma((planes,)),
+            pltpu.VMEM((planes, chunks, count + late, span), bf16),
+            pltpu.VMEM((planes + 1, chunks, count + late, span), bf16),
+            pltpu.VMEM((count + late, span), jnp.float32),
+            pltpu.VMEM((chunks, late, span), bf16),
+            dma((4,)), dma((ctx,)), dma((ctx,)), dma((planes, 2, pieces)),
+            dma((2, pieces)), dma((2, pieces)), dma((planes, 2, pieces)), dma((planes, pieces)), dma((planes,)), dma((planes,)),
             dma((planes, chunks)), dma((planes, chunks)), dma((planes, chunks)), dma((planes + 1, chunks)),
+            dma((chunks,)), dma((chunks,)),
         ],
         compiler_params=pltpu.CompilerParams(
             collective_id=0, has_side_effects=True, vmem_limit_bytes=60 * 1024 * 1024),
@@ -285,6 +331,8 @@
 
 TILE = 256
 SPAN = 512
+PIECES = 4
+LATE = 32
 
 
 def expert_half(rows, w_in, w_out):

time: 147 us -> 161 us (1.095)
  Pallas kernels: 143 us -> 158 us
    pallas_call x1, Pallas kernels: 143 us -> 158 us  [dense(): pl.pallas_call(functools.partial(layer_kernel, planes), out_shape=jax.Sha...]
where the time goes in v4:
time: 161 us
  Pallas kernels  158 us (98%)
  local copies, waits for them, and re-layouts  1.97 us (1%)
    pallas_call x1, Pallas kernels, dense(): pl.pallas_call(functools.partial(layer_kernel, planes), out_shape=jax.Sha...  158 us

profile of v4, /device:TPU:8, one launch (start us, length us, event | category | flops | bytes accessed | tf_op | source)
XLA Modules:
  0.0 160.9 jit_solution(12263946244166934272)
XLA Ops:
  0.0 1.3 select_reduce_fusion.gates_ref
  1.3 157.7 %experts.1 = bf16[128,2560]{1,0:T(8,128)(2,1)} custom-call(bf16[128,2560]{1,0:T(8,128)(2,1)} %tokens_hbm.1, f32[8,128]{1,0:T(8,128)} %select_reduce_fusion.gates_ref, bf16[1,2560,1536]{2,1,0:T(8,128)(2,1)} %w_in_hbm.1, bf16[1,768,2560]{2,1,0:T(8,128)(2,1)} %w_out_hbm.1), custom_call_target="tpu_custom_call" | custom-call | tf_op jit(solution)/shard_map/experts/pallas_call | solution.py:302
  159.0 2.0 %copy.7 = bf16[128,2560]{1,0:T(8,128)(2,1)} copy(bf16[128,2560]{1,0:T(8,128)(2,1)} %experts.1) | data formatting | bytes 1310720

commit v5 on v3

--- a/solution.py
+++ b/solution.py
@@ -191,7 +191,7 @@
         def _(chunk):
             back_copy(step, chunk).start()
 
-    for step in [planes - 2] * (planes > 2) + [planes - 1] * (planes > 1) + list(range(planes - 3, 0, -1)):
+    for step in range(planes - 1, 0, -1):
         reduce(step)
 
     @pl.loop(0, chunks)

time: 147 us -> 134 us (0.912)
  Pallas kernels: 143 us -> 129 us
    pallas_call x1, Pallas kernels: 143 us -> 129 us  [dense(): pl.pallas_call(functools.partial(layer_kernel, planes), out_shape=jax.Sha...]
where the time goes in v5:
time: 134 us; the launch traced here: 132 us
  Pallas kernels  129 us (96%)
  local copies, waits for them, and re-layouts  1.97 us (1%)
    pallas_call x1, Pallas kernels, dense(): pl.pallas_call(functools.partial(layer_kernel, planes), out_shape=jax.Sha...  129 us

profile of v5, /device:TPU:8, one launch (start us, length us, event | category | flops | bytes accessed | tf_op | source)
XLA Modules:
  0.0 132.4 jit_solution(4208054867105519301)
XLA Ops:
  0.0 1.3 select_reduce_fusion.gates_ref
  1.3 129.1 %experts.1 = bf16[128,2560]{1,0:T(8,128)(2,1)} custom-call(bf16[128,2560]{1,0:T(8,128)(2,1)} %tokens_hbm.1, f32[8,128]{1,0:T(8,128)} %select_reduce_fusion.gates_ref, bf16[1,2560,1536]{2,1,0:T(8,128)(2,1)} %w_in_hbm.1, bf16[1,768,2560]{2,1,0:T(8,128)(2,1)} %w_out_hbm.1), custom_call_target="tpu_custom_call" | custom-call | tf_op jit(solution)/shard_map/experts/pallas_call | solution.py:258
  130.4 2.0 %copy.7 = bf16[128,2560]{1,0:T(8,128)(2,1)} copy(bf16[128,2560]{1,0:T(8,128)(2,1)} %experts.1) | data formatting | bytes 1310720
